TPU v7x, 512 devices: a whole 4x8x8 slice. The times are simulated.
512 devices in a mesh: dp: 128 (over y, z, core), rep: 4 (over x).
Axes of the slice: x: 4, y: 8, z: 8, core: 2. Of those that a mesh axis runs over, the one named last changes fastest.
Arguments:
- gradient_receptance: bfloat16 [128, 4, 2, 768, 768], P('dp', 'rep'), may hold values from -1000 to 1000
- gradient_factors: bfloat16 [128, 4, 2, 768, 256], P('dp', 'rep'), may hold values from -1000 to 1000
- gradient_channels: bfloat16 [128, 4, 2, 768, 16], P('dp', 'rep'), may hold values from -1000 to 1000
- primary_receptance: float32 [768, 768], P('dp'), may hold values from -0.21875 to 0.21875
- primary_factors: float32 [768, 256], P('dp'), may hold values from -0.21875 to 0.21875
- primary_channels: float32 [768, 16], P('dp'), may hold values from -1 to 1
- first_moment_receptance: float32 [768, 768], P('dp'), may hold values from -0.00390625 to 0.00390625
- first_moment_factors: float32 [768, 256], P('dp'), may hold values from -0.00390625 to 0.00390625
- first_moment_channels: float32 [768, 16], P('dp'), may hold values from -0.00390625 to 0.00390625
- second_moment_receptance: float32 [768, 768], P('dp'), may hold values from 1e-08 to 1e-06
- second_moment_factors: float32 [768, 256], P('dp'), may hold values from 1e-08 to 1e-06
- second_moment_channels: float32 [768, 16], P('dp'), may hold values from 1e-08 to 1e-06
Outputs:
- weight_receptance: bfloat16 [768, 768], replicated
- weight_lora: bfloat16 [768, 256], replicated
- weight_vectors: bfloat16 [768, 16], replicated
- new_master_receptance: float32 [768, 768], P('dp')
- new_master_lora: float32 [768, 256], P('dp')
- new_master_vectors: float32 [768, 16], P('dp')
- new_first_receptance: float32 [768, 768], P('dp')
- new_first_lora: float32 [768, 256], P('dp')
- new_first_vectors: float32 [768, 16], P('dp')
- new_second_receptance: float32 [768, 768], P('dp')
- new_second_lora: float32 [768, 256], P('dp')
- new_second_vectors: float32 [768, 16], P('dp')
All inputs are finite; a program needn't handle non-finite values.
Results may differ from a plain program's by a relative error of at most 0.001.
Values may be sent and summed in bfloat16 or wider, within the bound.
A program may use at most 64 MiB of HBM per device.

v0:
```python
import jax
import jax.numpy as jnp
from jax import lax
from jax.sharding import PartitionSpec as P

STEP = 20
beta_one = 0.9
beta_two = 0.99
adam_eps = 1e-08
learn_rate = 0.001
weight_decay_rate = 0.1
max_norm = 1.0
norm_eps = 1e-06


def decoupled_adam_step(gradient, master, first, second, decay):
    new_first = beta_one * first + (1.0 - beta_one) * gradient
    new_second = beta_two * second + (1.0 - beta_two) * gradient * gradient
    update = (
        new_first
        / (1.0 - beta_one**STEP)
        / (jnp.sqrt(new_second / (1.0 - beta_two**STEP)) + adam_eps)
    )
    new_master = master - learn_rate * (update + decay * master)
    return (new_master, new_first, new_second)


def body(
    gradient_receptance,
    gradient_factors,
    gradient_channels,
    primary_receptance,
    primary_factors,
    primary_channels,
    first_moment_receptance,
    first_moment_factors,
    first_moment_channels,
    second_moment_receptance,
    second_moment_factors,
    second_moment_channels,
):
    row_count = primary_receptance.shape[0]
    receptance_width = primary_receptance.shape[1]
    factor_width = primary_factors.shape[1]
    local_sum = jnp.concatenate(
        [
            jnp.sum(gradient_receptance, axis=(0, 1, 2), dtype=jnp.float32),
            jnp.sum(gradient_factors, axis=(0, 1, 2), dtype=jnp.float32),
            jnp.sum(gradient_channels, axis=(0, 1, 2), dtype=jnp.float32),
        ],
        axis=1,
    )
    full_sum = lax.psum(local_sum, ("dp", "rep"))
    square_sum = jnp.sum(full_sum * full_sum)
    owned_rows = lax.dynamic_slice_in_dim(full_sum, lax.axis_index("dp") * row_count, row_count, 0)
    clipping_ratio = jnp.minimum(1.0, max_norm / (jnp.sqrt(square_sum) + norm_eps))
    gradient_clipped = clipping_ratio * owned_rows
    separate_factors = receptance_width + factor_width
    receptance_part = decoupled_adam_step(
        gradient_clipped[:, :receptance_width],
        primary_receptance,
        first_moment_receptance,
        second_moment_receptance,
        weight_decay_rate,
    )
    lowrank_factors = decoupled_adam_step(
        gradient_clipped[:, receptance_width:separate_factors],
        primary_factors,
        first_moment_factors,
        second_moment_factors,
        weight_decay_rate,
    )
    channel_vectors = decoupled_adam_step(
        gradient_clipped[:, separate_factors:],
        primary_channels,
        first_moment_channels,
        second_moment_channels,
        0.0,
    )
    packed_gradients = jnp.concatenate(
        [receptance_part[0], lowrank_factors[0], channel_vectors[0]], axis=1
    ).astype(jnp.bfloat16)
    collected_parts = lax.all_gather(packed_gradients, "dp", axis=0, tiled=True)
    return (
        collected_parts[:, :receptance_width],
        collected_parts[:, receptance_width:separate_factors],
        collected_parts[:, separate_factors:],
        receptance_part[0],
        lowrank_factors[0],
        channel_vectors[0],
        receptance_part[1],
        lowrank_factors[1],
        channel_vectors[1],
        receptance_part[2],
        lowrank_factors[2],
        channel_vectors[2],
    )


def solution(mesh):
    placed = (
        P("dp", "rep", None, None, None),
        P("dp", "rep", None, None, None),
        P("dp", "rep", None, None, None),
        P("dp", None),
        P("dp", None),
        P("dp", None),
        P("dp", None),
        P("dp", None),
        P("dp", None),
        P("dp", None),
        P("dp", None),
        P("dp", None),
    )
    return jax.shard_map(
        body,
        mesh=mesh,
        in_specs=placed,
        out_specs=(
            P(),
            P(),
            P(),
            P("dp", None),
            P("dp", None),
            P("dp", None),
            P("dp", None),
            P("dp", None),
            P("dp", None),
            P("dp", None),
            P("dp", None),
            P("dp", None),
        ),
        check_vma=False,
    )
```

profile of v0, /device:TPU:1, one launch (start us, length us, event | category | flops | bytes accessed | tf_op | source)
XLA Modules:
  0.0 402.7 jit_solution(3003062648250207814)
XLA Ops:
  7.2 0.0 all-reduce.2.cloned.1.call-start
  7.2 0.8 convert_reduce_fusion.2
  8.0 0.2 copy.26
  8.2 1.3 convert_reduce_fusion.1
  9.5 2.3 convert_reduce_fusion
  11.9 2.0 pad_maximum_fusion
  13.9 0.0 copy-start.4
  13.9 0.0 copy-start
  13.9 0.0 copy-start.1
  14.0 0.0 all-reduce.2.cloned.1.call-update
  14.0 0.0 all-gather.3.cloned.1.call-start
  14.1 288.3 %all-reduce.2.cloned.1.call-done = f32[768,1040]{1,0:T(8,128)} async-done(((f32[768,1040]{1,0:T(8,128)}), f32[768,1040]{1,0:T(8,128)}) %all-reduce.2.cloned.1.call-update) | async-done | bytes 3194896 | tf_op jit(solution)/shard_map/psum | solution.py:53
  302.3 3.5 multiply_reduce_fusion
  306.6 0.9 dynamic-slice_multiply_fusion
  307.5 0.6 fusion.7
  308.2 0.6 fusion.5
  308.8 0.6 fusion.3
  309.4 0.6 maximum_bitcast_fusion
  310.0 0.0 all-gather.3.cloned.1.call-update
  310.1 80.3 %all-gather.3.cloned.1.call-done = bf16[128,6,1040]{2,1,0:T(8,128)(2,1)} async-done(((bf16[1,6,1040]{2,1,0:T(8,128)(2,1)}), bf16[128,6,1040]{2,1,0:T(8,128)(2,1)}) %all-gather.3.cloned.1.call-update) | async-done | bytes 1597456 | tf_op jit(solution)/shard_map/all_gather | solution.py:83
  390.3 3.0 reshape.25
  393.3 1.1 slice.27
  394.4 0.8 slice.28
  395.2 0.7 copy.27
  (16 shorter events, 0.0 us)
Async XLA Ops:
  7.2 295.2 %all-reduce.2.cloned.1.call-start = ((), (), s32[]{:S(2)}) async-start(), calls=%async_computation | async-start | bytes 7077888 | tf_op jit(solution)/shard_map/psum | solution.py:53
  13.9 293.6 %copy-start.6 = (f32[6,16]{1,0:T(8,128)S(1)}, f32[6,16]{1,0:T(8,128)}, u32[]{:S(2)}) copy-start(f32[6,16]{1,0:T(8,128)} %param.17) | copy-start | bytes 1156
  13.9 293.6 %copy-start.7 = (f32[6,16]{1,0:T(8,128)S(1)}, f32[6,16]{1,0:T(8,128)}, u32[]{:S(2)}) copy-start(f32[6,16]{1,0:T(8,128)} %param.20) | copy-start | bytes 1156
  13.9 293.6 %copy-start.8 = (f32[6,16]{1,0:T(8,128)S(1)}, f32[6,16]{1,0:T(8,128)}, u32[]{:S(2)}) copy-start(f32[6,16]{1,0:T(8,128)} %param.23) | copy-start | bytes 1156
  13.9 294.2 %copy-start.3 = (f32[6,256]{1,0:T(8,128)S(1)}, f32[6,256]{1,0:T(8,128)}, u32[]{:S(2)}) copy-start(f32[6,256]{1,0:T(8,128)} %param.16) | copy-start | bytes 18436
  13.9 294.2 %copy-start.4 = (f32[6,256]{1,0:T(8,128)S(1)}, f32[6,256]{1,0:T(8,128)}, u32[]{:S(2)}) copy-start(f32[6,256]{1,0:T(8,128)} %param.19) | copy-start | bytes 18436
  13.9 294.2 %copy-start.5 = (f32[6,256]{1,0:T(8,128)S(1)}, f32[6,256]{1,0:T(8,128)}, u32[]{:S(2)}) copy-start(f32[6,256]{1,0:T(8,128)} %param.22) | copy-start | bytes 18436
  13.9 294.8 %copy-start = (f32[6,768]{1,0:T(8,128)S(1)}, f32[6,768]{1,0:T(8,128)}, u32[]{:S(2)}) copy-start(f32[6,768]{1,0:T(8,128)} %param.15) | copy-start | bytes 55300
  13.9 294.8 %copy-start.1 = (f32[6,768]{1,0:T(8,128)S(1)}, f32[6,768]{1,0:T(8,128)}, u32[]{:S(2)}) copy-start(f32[6,768]{1,0:T(8,128)} %param.18) | copy-start | bytes 55300
  14.0 294.8 %copy-start.2 = (f32[6,768]{1,0:T(8,128)S(1)}, f32[6,768]{1,0:T(8,128)}, u32[]{:S(2)}) copy-start(f32[6,768]{1,0:T(8,128)} %param.21) | copy-start | bytes 55300
  14.0 376.3 %all-gather.3.cloned.1.call-start = ((), (), s32[]{:S(2)}) async-start(), calls=%async_computation.1 | async-start | bytes 2377728 | tf_op jit(solution)/shard_map/all_gather | solution.py:83
Sparse Core Ops, SparseCore 0:
  14.1 288.1 all-reduce.1
  310.2 80.0 all-gather.2
where the time goes:
time: 403 us
  waiting for transfers between devices  369 us (92%)
  between operations  14.9 us (4%)
  other arithmetic  13.4 us (3%)
  local copies, waits for them, and re-layouts  5.78 us (1%)
    psum x1, waiting for transfers between devices, body(): full_sum = lax.psum(local_sum, ('dp', 'rep'))  288 us
    all_gather x1, waiting for transfers between devices, body(): collected_parts = lax.all_gather(packed_gradients, 'dp', axis=0, tiled=True)  80.3 us
  transfers between devices with their start and end apart: 2, of which 2 were waited for; matrix products, arithmetic and copies ran while one was open for 0% of the time, Pallas kernels for 0%

commit v1 on v0

--- a/solution.py
+++ b/solution.py
@@ -50,7 +50,7 @@
         ],
         axis=1,
     )
-    full_sum = lax.psum(local_sum, ("dp", "rep"))
+    full_sum = lax.psum(lax.psum(local_sum, "dp"), "rep")
     square_sum = jnp.sum(full_sum * full_sum)
     owned_rows = lax.dynamic_slice_in_dim(full_sum, lax.axis_index("dp") * row_count, row_count, 0)
     clipping_ratio = jnp.minimum(1.0, max_norm / (jnp.sqrt(square_sum) + norm_eps))

time: 403 us -> 420 us (1.042)
  waiting for transfers between devices: 369 us -> 386 us
    psum x1 -> x2, waiting for transfers between devices: 288 us -> 302 us  [body(): full_sum = lax.psum(lax.psum(local_sum, 'dp'), 'rep')]
  transfers between devices with their start and end apart: 2 -> 3, of which waited for: 2 -> 3; matrix products, arithmetic and copies ran while one was open for 0% -> 0% of each run, Pallas kernels for 0% -> 0%
where the time goes in v1:
time: 420 us
  waiting for transfers between devices  386 us (92%)
  between operations  14.6 us (3%)
  other arithmetic  13.4 us (3%)
  local copies, waits for them, and re-layouts  5.78 us (1%)
    psum x2, waiting for transfers between devices, body(): full_sum = lax.psum(lax.psum(local_sum, 'dp'), 'rep')  302 us
    all_gather x1, waiting for transfers between devices, body(): collected_parts = lax.all_gather(packed_gradients, 'dp', axis=0, tiled=True)  83.7 us
  transfers between devices with their start and end apart: 3, of which 3 were waited for; matrix products, arithmetic and copies ran while one was open for 0% of the time, Pallas kernels for 0%

profile of v1, /device:TPU:1, one launch (start us, length us, event | category | flops | bytes accessed | tf_op | source)
XLA Modules:
  0.0 420.1 jit_solution(16020408282837141847)
XLA Ops:
  7.2 0.0 all-reduce.3.cloned.1.call-start
  7.2 0.8 convert_reduce_fusion.2
  8.0 0.2 copy.26
  8.2 1.3 convert_reduce_fusion.1
  9.5 2.3 convert_reduce_fusion
  11.9 2.0 pad_maximum_fusion
  13.9 0.0 all-reduce.3.cloned.1.call-update
  13.9 0.0 all-reduce.5.cloned.1.call-start
  14.0 209.4 %all-reduce.3.cloned.1.call-done = f32[768,1040]{1,0:T(8,128)} async-done(((f32[768,1040]{1,0:T(8,128)}), f32[768,1040]{1,0:T(8,128)}) %all-reduce.3.cloned.1.call-update) | async-done | bytes 3194896 | tf_op jit(solution)/shard_map/psum | solution.py:53
  223.4 0.0 all-reduce.5.cloned.1.call-update
  223.4 0.0 all-gather.3.cloned.1.call-start
  223.5 93.0 %all-reduce.5.cloned.1.call-done = f32[768,1040]{1,0:T(8,128)} async-done(((f32[768,1040]{1,0:T(8,128)}), f32[768,1040]{1,0:T(8,128)}) %all-reduce.5.cloned.1.call-update) | async-done | bytes 3194896 | tf_op jit(solution)/shard_map/psum | solution.py:53
  316.5 3.5 multiply_reduce_fusion
  320.8 0.9 dynamic-slice_multiply_fusion
  321.7 0.6 fusion.7
  322.3 0.6 fusion.5
  323.0 0.6 fusion.3
  323.6 0.6 maximum_bitcast_fusion
  324.2 0.0 all-gather.3.cloned.1.call-update
  324.2 83.7 %all-gather.3.cloned.1.call-done = bf16[128,6,1040]{2,1,0:T(8,128)(2,1)} async-done(((bf16[1,6,1040]{2,1,0:T(8,128)(2,1)}), bf16[128,6,1040]{2,1,0:T(8,128)(2,1)}) %all-gather.3.cloned.1.call-update) | async-done | bytes 1597456 | tf_op jit(solution)/shard_map/all_gather | solution.py:83
  408.0 3.0 reshape.25
  411.0 1.1 slice.27
  412.1 0.8 slice.28
  412.8 0.7 copy.27
  (19 shorter events, 0.1 us)
Async XLA Ops:
  7.2 216.2 %all-reduce.3.cloned.1.call-start = ((), (), s32[]{:S(2)}) async-start(), calls=%async_computation | async-start | bytes 7077888 | tf_op jit(solution)/shard_map/psum | solution.py:53
  13.9 302.6 %all-reduce.5.cloned.1.call-start = ((), (), s32[]{:S(2)}) async-start(), calls=%async_computation.1 | async-start | bytes 7077888 | tf_op jit(solution)/shard_map/psum | solution.py:53
  223.3 98.3 %copy-start.6 = (f32[6,16]{1,0:T(8,128)S(1)}, f32[6,16]{1,0:T(8,128)}, u32[]{:S(2)}) copy-start(f32[6,16]{1,0:T(8,128)} %param.17) | copy-start | bytes 1156
  223.3 98.3 %copy-start.7 = (f32[6,16]{1,0:T(8,128)S(1)}, f32[6,16]{1,0:T(8,128)}, u32[]{:S(2)}) copy-start(f32[6,16]{1,0:T(8,128)} %param.20) | copy-start | bytes 1156
  223.3 98.3 %copy-start.8 = (f32[6,16]{1,0:T(8,128)S(1)}, f32[6,16]{1,0:T(8,128)}, u32[]{:S(2)}) copy-start(f32[6,16]{1,0:T(8,128)} %param.23) | copy-start | bytes 1156
  223.3 99.0 %copy-start.3 = (f32[6,256]{1,0:T(8,128)S(1)}, f32[6,256]{1,0:T(8,128)}, u32[]{:S(2)}) copy-start(f32[6,256]{1,0:T(8,128)} %param.16) | copy-start | bytes 18436
  223.4 99.0 %copy-start.4 = (f32[6,256]{1,0:T(8,128)S(1)}, f32[6,256]{1,0:T(8,128)}, u32[]{:S(2)}) copy-start(f32[6,256]{1,0:T(8,128)} %param.19) | copy-start | bytes 18436
  223.4 99.0 %copy-start.5 = (f32[6,256]{1,0:T(8,128)S(1)}, f32[6,256]{1,0:T(8,128)}, u32[]{:S(2)}) copy-start(f32[6,256]{1,0:T(8,128)} %param.22) | copy-start | bytes 18436
  223.4 99.6 %copy-start = (f32[6,768]{1,0:T(8,128)S(1)}, f32[6,768]{1,0:T(8,128)}, u32[]{:S(2)}) copy-start(f32[6,768]{1,0:T(8,128)} %param.15) | copy-start | bytes 55300
  223.4 99.6 %copy-start.1 = (f32[6,768]{1,0:T(8,128)S(1)}, f32[6,768]{1,0:T(8,128)}, u32[]{:S(2)}) copy-start(f32[6,768]{1,0:T(8,128)} %param.18) | copy-start | bytes 55300
  223.4 99.6 %copy-start.2 = (f32[6,768]{1,0:T(8,128)S(1)}, f32[6,768]{1,0:T(8,128)}, u32[]{:S(2)}) copy-start(f32[6,768]{1,0:T(8,128)} %param.21) | copy-start | bytes 55300
  223.4 184.6 %all-gather.3.cloned.1.call-start = ((), (), s32[]{:S(2)}) async-start(), calls=%async_computation.2 | async-start | bytes 2377728 | tf_op jit(solution)/shard_map/all_gather | solution.py:83
Sparse Core Ops, SparseCore 0:
  14.0 209.2 all-reduce.2
  225.7 90.7 all-reduce.4
  324.4 83.5 all-gather.2
